TPU v7x, 256 devices: a whole 4x4x8 slice. The times are simulated.
256 devices in a mesh: row: 8 (over x_hi, y), col: 16 (over x_lo, z), depth: 2 (over core).
Axes of the slice: x: 4 (x_hi: 2, x_lo: 2; x = x_hi * 2 + x_lo), y: 4, z: 8, core: 2. Of those that a mesh axis runs over, the one named last changes fastest.
Arguments:
- snapshots: bfloat16 [8192, 6144], P('col', ('row', 'depth')), may hold values from -6 to 6
- cell_weight: float32 [6144], P(('row', 'depth')), may hold values from 0.25 to 4
Outputs:
- gram: float32 [8192, 8192], P('row', ('col', 'depth'))
All inputs are finite; a program needn't handle non-finite values.
Results may differ from a plain program's by a relative error of at most 0.0034.
Values may be sent and summed in bfloat16 or wider, within the bound.
A program may use at most 64 MiB of HBM per device.

v0:
```python
import jax
import jax.numpy as jnp
from jax import lax
from jax.sharding import PartitionSpec as P

CELLS = 6144


def spread(value, axis, root):
    mine = lax.axis_index(axis) == root
    return lax.psum(jnp.where(mine, value, jnp.zeros_like(value)), axis)


def block_product(left_rows, right_rows):
    return lax.dot_general(
        left_rows, right_rows, (((1,), (1,)), ((), ())), preferred_element_type=jnp.float32
    )


def on_device(snapshots, cell_weight):
    root_weight = jnp.sqrt(cell_weight)
    scaled = (snapshots.astype(jnp.float32) * root_weight[None, :]).astype(jnp.bfloat16)
    ratio = lax.axis_size("col") // lax.axis_size("row")
    row_index = lax.axis_index("row")
    own_half = lax.all_to_all(scaled, "depth", split_axis=0, concat_axis=1, tiled=True)
    column_rows = lax.all_gather(own_half, "row", axis=1, tiled=True)
    blocks = []
    for offset in range(ratio):
        received = spread(column_rows, "col", row_index * ratio + offset)
        panel = lax.all_gather(received, "depth", axis=0, tiled=True)
        blocks.append(block_product(panel, column_rows))
    summed = jnp.concatenate(blocks, axis=0)
    return summed / jnp.float32(CELLS)


def solution(mesh):
    return jax.shard_map(
        on_device,
        mesh=mesh,
        in_specs=(P("col", ("row", "depth")), P(("row", "depth"))),
        out_specs=P("row", ("col", "depth")),
        check_vma=False,
    )
```

profile of v0, /device:TPU:1, one launch (start us, length us, event | category | flops | bytes accessed | tf_op | source)
XLA Modules:
  0.0 312.5 jit_solution(17423698580459638901)
XLA Ops:
  6.5 0.0 all-gather.4.cloned.1.call-start
  6.5 0.7 sqrt.3
  7.2 1.1 multiply_convert_fusion
  8.3 6.9 %all_to_all.19 = bf16[2,256,384]{2,1,0:T(8,128)(2,1)S(1)} all-to-all(bf16[2,256,384]{2,1,0:T(8,128)(2,1)S(1)} %bitcast.8), channel_id=1, replica_groups=mesh['row'=8,'col'=16,'depth'=2] {'depth'}, dimensions={0} | all-to-all | bytes 786432 | tf_op jit(solution)/shard_map/all_to_all | solution.py:25
  15.2 0.9 copy.3
  16.1 0.0 all-gather.4.cloned.1.call-update
  16.2 0.0 all-reduce.3.cloned.1.call-start
  16.2 68.3 %all-gather.4.cloned.1.call-done = bf16[256,6144]{0,1:T(8,128)(2,1)} async-done(((bf16[256,768]{0,1:T(8,128)(2,1)}), bf16[256,6144]{0,1:T(8,128)(2,1)}) %all-gather.4.cloned.1.call-update) | async-done | bytes 3145744 | tf_op jit(solution)/shard_map/all_gather | solution.py:26
  84.6 4.9 %broadcast_select_fusion.1 = (bf16[256,6144]{0,1:T(8,128)(2,1)}, bf16[256,6144]{0,1:T(8,128)(2,1)}) fusion(bf16[256,6144]{0,1:T(8,128)(2,1)} %all-gather.4.cloned.1.call-done, pred[]{:T(512)S(6)} %eq.6, pred[]{:T(512)S(6)} %eq.7), kind=kLoop, calls=%fused_computation.1 | loop fusion | flops 3145728 | bytes 9437186 | tf_op jit(solution)/shard_map/jit(_where)/select_n | solution.py:11
  89.5 0.0 all-reduce.3.cloned.1.call-update
  89.5 0.0 all-gather.8.cloned.1.call-start
  89.6 162.2 %all-reduce.3.cloned.1.call-done = (bf16[256,6144]{0,1:T(8,128)(2,1)}, bf16[256,6144]{0,1:T(8,128)(2,1)}) async-done(((bf16[256,6144]{0,1:T(8,128)(2,1)}, bf16[256,6144]{0,1:T(8,128)(2,1)}), (bf16[256,6144]{0,1:T(8,128)(2,1)}, bf16[256,6144]{0,1:T(8,128)(2,1)})) %all-reduce.3.cloned.1.call-update) | async-done | bytes 6291472 | tf_op jit(solution)/shard_map/psum | solution.py:11
  251.7 0.0 copy-start
  251.7 0.0 all-gather.8.cloned.1.call-update
  251.8 0.0 all-gather.6.cloned.1.call-start
  251.8 0.5 all-gather.6.cloned.1.call-update
  252.3 23.9 %all-gather.8.cloned.1.call-done = bf16[512,6144]{0,1:T(8,128)(2,1)} async-done(((bf16[256,6144]{0,1:T(8,128)(2,1)}), bf16[512,6144]{0,1:T(8,128)(2,1)}) %all-gather.8.cloned.1.call-update) | async-done | bytes 6291472 | tf_op jit(solution)/shard_map/all_gather | solution.py:30
  276.3 0.0 copy-done
  276.3 5.4 %fusion.1 = f32[512,256]{1,0:T(8,128)} fusion(bf16[512,6144]{0,1:T(8,128)(2,1)} %all-gather.8.cloned.1.call-done, bf16[256,6144]{0,1:T(8,128)(2,1)S(1)} %copy-done), kind=kOutput, calls=%fused_computation.5 | convolution fusion | flops 1610612736 | bytes 9961472 | tf_op jit(solution)/shard_map/dot_general | solution.py:15
  281.7 18.6 %all-gather.6.cloned.1.call-done = bf16[512,6144]{0,1:T(8,128)(2,1)} async-done(((bf16[256,6144]{0,1:T(8,128)(2,1)}), bf16[512,6144]{0,1:T(8,128)(2,1)}) %all-gather.6.cloned.1.call-update) | async-done | bytes 6291472 | tf_op jit(solution)/shard_map/all_gather | solution.py:30
  300.2 0.0 copy-start.1
  300.2 4.7 %fusion = f32[512,256]{1,0:T(8,128)S(1)} fusion(bf16[512,6144]{0,1:T(8,128)(2,1)} %all-gather.6.cloned.1.call-done, bf16[256,6144]{0,1:T(8,128)(2,1)S(1)} %copy-done), kind=kOutput, calls=%fused_computation.4 | convolution fusion | flops 1610612736 | bytes 9961472 | tf_op jit(solution)/shard_map/dot_general | solution.py:15
  304.9 0.0 copy-done.1
  304.9 1.1 maximum_multiply_fusion
Async XLA Ops:
  6.5 78.0 %all-gather.4.cloned.1.call-start = ((), (), s32[]{:S(2)}) async-start(), calls=%async_computation.1 | async-start | bytes 3538944 | tf_op jit(solution)/shard_map/all_gather | solution.py:26
  16.2 235.6 %all-reduce.3.cloned.1.call-start = ((), (), s32[]{:S(2)}) async-start(), calls=%async_computation.4 | async-start | bytes 12582912 | tf_op jit(solution)/shard_map/psum | solution.py:11
  89.5 186.7 %all-gather.8.cloned.1.call-start = ((), (), s32[]{:S(2)}) async-start(), calls=%async_computation.3 | async-start | bytes 9437184 | tf_op jit(solution)/shard_map/all_gather | solution.py:30
  251.7 24.5 %copy-start = (bf16[256,6144]{0,1:T(8,128)(2,1)S(1)}, bf16[256,6144]{0,1:T(8,128)(2,1)}, u32[]{:S(2)}) copy-start(bf16[256,6144]{0,1:T(8,128)(2,1)} %all-gather.4.cloned.1.call-done) | copy-start | bytes 9437188
  251.8 48.5 %all-gather.6.cloned.1.call-start = ((), (), s32[]{:S(2)}) async-start(), calls=%async_computation.2 | async-start | bytes 9437184 | tf_op jit(solution)/shard_map/all_gather | solution.py:30
  300.2 4.7 %copy-start.1 = (f32[512,256]{1,0:T(8,128)S(1)}, f32[512,256]{1,0:T(8,128)}, u32[]{:S(2)}) copy-start(f32[512,256]{1,0:T(8,128)} %fusion.1) | copy-start | bytes 1572868
Sparse Core Ops, SparseCore 0:
  16.3 68.2 all-gather.3
  89.6 162.0 all-reduce.2
  253.5 22.6 all-gather.7
  277.9 22.2 all-gather.5
where the time goes:
time: 313 us
  waiting for transfers between devices  274 us (88%)
  between operations  13.2 us (4%)
  matrix products  10.1 us (3%)
  other arithmetic  7.09 us (2%)
  blocking collectives  6.92 us (2%)
    psum x1, waiting for transfers between devices, spread(): return lax.psum(jnp.where(mine, value, jnp.zeros_like(value)), axis)  162 us
    all_gather x1, waiting for transfers between devices, on_device(): column_rows = lax.all_gather(own_half, 'row', axis=1, tiled=True)  68.3 us
    all_gather x2, waiting for transfers between devices, on_device(): panel = lax.all_gather(received, 'depth', axis=0, tiled=True)  42.5 us
    dot_general x2, matrix products, block_product(): lax.dot_general(left_rows, right_rows, (((1,), (1,)), ((), ())), preferre...  10.1 us
    all_to_all x1, blocking collectives, on_device(): lax.all_to_all(scaled, 'depth', split_axis=0, concat_axis=1, tiled=True)  6.92 us
  transfers between devices with their start and end apart: 4, of which 4 were waited for; matrix products, arithmetic and copies ran while one was open for 2% of the time, Pallas kernels for 0%

commit v1 on v0

--- a/solution.py
+++ b/solution.py
@@ -4,6 +4,13 @@
 from jax.sharding import PartitionSpec as P
 
 CELLS = 6144
+
+
+def exchange_gather(x, axis, dim):
+    size = lax.axis_size(axis)
+    pieces = jnp.stack([x for _ in range(size)])
+    pieces = lax.all_to_all(pieces, axis, split_axis=0, concat_axis=0)
+    return jnp.concatenate(pieces, axis=dim)
 
 
 def spread(value, axis, root):
@@ -23,7 +30,7 @@
     ratio = lax.axis_size("col") // lax.axis_size("row")
     row_index = lax.axis_index("row")
     own_half = lax.all_to_all(scaled, "depth", split_axis=0, concat_axis=1, tiled=True)
-    column_rows = lax.all_gather(own_half, "row", axis=1, tiled=True)
+    column_rows = exchange_gather(own_half, "row", 1)
     blocks = []
     for offset in range(ratio):
         received = spread(column_rows, "col", row_index * ratio + offset)

time: 313 us -> 293 us (0.936)
  waiting for transfers between devices: 274 us -> 246 us
  starting transfers between devices: 0.12 us -> 5.03 us
  local copies, waits for them, and re-layouts: 1.62 us -> 6.08 us
    all_gather x1 -> x0, waiting for transfers between devices: 68.3 us -> none  [on_device(): column_rows = lax.all_gather(own_half, 'row', axis=1, tiled=True)]
    all_to_all x0 -> x1, waiting for transfers between devices: none -> 37.5 us  [exchange_gather(): pieces = lax.all_to_all(pieces, axis, split_axis=0, concat_axis=0)]
    all_to_all x0 -> x1, starting transfers between devices: none -> 4.91 us  [exchange_gather(): pieces = lax.all_to_all(pieces, axis, split_axis=0, concat_axis=0)]
    all_to_all x0 -> x1, local copies, waits for them, and re-layouts: none -> 3.17 us  [exchange_gather(): pieces = lax.all_to_all(pieces, axis, split_axis=0, concat_axis=0)]
where the time goes in v1:
time: 293 us; the launch traced here: 292 us
  waiting for transfers between devices  246 us (84%)
  between operations  13.2 us (5%)
  matrix products  10.1 us (3%)
  blocking collectives  6.92 us (2%)
  local copies, waits for them, and re-layouts  6.08 us (2%)
  other arithmetic  5.41 us (2%)
  starting transfers between devices  5.03 us (2%)
    psum x1, waiting for transfers between devices, spread(): return lax.psum(jnp.where(mine, value, jnp.zeros_like(value)), axis)  165 us
    all_gather x2, waiting for transfers between devices, on_device(): panel = lax.all_gather(received, 'depth', axis=0, tiled=True)  42.5 us
    all_to_all x1, waiting for transfers between devices, exchange_gather(): pieces = lax.all_to_all(pieces, axis, split_axis=0, concat_axis=0)  37.5 us
    dot_general x2, matrix products, block_product(): lax.dot_general(left_rows, right_rows, (((1,), (1,)), ((), ())), preferre...  10.1 us
    all_to_all x1, blocking collectives, on_device(): lax.all_to_all(scaled, 'depth', split_axis=0, concat_axis=1, tiled=True)  6.92 us
  transfers between devices with their start and end apart: 4, of which 4 were waited for; matrix products, arithmetic and copies ran while one was open for 2% of the time, Pallas kernels for 0%

profile of v1, /device:TPU:1, one launch (start us, length us, event | category | flops | bytes accessed | tf_op | source)
XLA Modules:
  0.0 292.4 jit_solution(4409419903419167150)
XLA Ops:
  6.5 0.7 sqrt.3
  7.2 1.1 multiply_convert_fusion
  8.3 6.9 %all_to_all.21 = bf16[2,256,384]{2,1,0:T(8,128)(2,1)S(1)} all-to-all(bf16[2,256,384]{2,1,0:T(8,128)(2,1)S(1)} %bitcast.14), channel_id=1, replica_groups=mesh['row'=8,'col'=16,'depth'=2] {'depth'}, dimensions={0} | all-to-all | bytes 786432 | tf_op jit(solution)/shard_map/all_to_all | solution.py:32
  15.2 0.2 copy.8
  15.4 0.2 copy.9
  15.6 1.9 stack.5
  17.5 4.9 %all-to-all-start.1 = ((bf16[8,256,768]{2,1,0:T(8,128)(2,1)}), bf16[8,256,768]{2,1,0:T(8,128)(2,1)}, u32[]{:S(2)}, u32[]{:S(2)}) async-start(bf16[8,256,768]{2,1,0:T(8,128)(2,1)} %stack.5), calls=%async_computation.1 | async-start | bytes 6291456 | tf_op jit(solution)/shard_map/all_to_all | solution.py:12
  22.4 0.0 all-reduce.3.cloned.1.call-start
  22.4 37.5 %all-to-all-done.1 = bf16[8,256,768]{2,1,0:T(8,128)(2,1)} async-done(((bf16[8,256,768]{2,1,0:T(8,128)(2,1)}), bf16[8,256,768]{2,1,0:T(8,128)(2,1)}, u32[]{:S(2)}, u32[]{:S(2)}) %all-to-all-start.1) | async-done | bytes 3145760 | tf_op jit(solution)/shard_map/all_to_all | solution.py:12
  59.9 3.2 %copy.10 = bf16[8,256,768]{1,2,0:T(8,128)(2,1)S(1)} copy(bf16[8,256,768]{2,1,0:T(8,128)(2,1)} %all-to-all-done.1) | data formatting | bytes 6291456 | tf_op jit(solution)/shard_map/all_to_all | solution.py:12
  63.1 3.3 %broadcast_select_fusion.1 = (bf16[256,6144]{0,1:T(8,128)(2,1)}, bf16[256,6144]{0,1:T(8,128)(2,1)}) fusion(pred[]{:T(512)S(6)} %eq.6, bf16[8,256,768]{1,2,0:T(8,128)(2,1)S(1)} %copy.10, pred[]{:T(512)S(6)} %eq.7), kind=kLoop, calls=%fused_computation.1 | loop fusion | flops 3145728 | bytes 9437186 | tf_op jit(solution)/shard_map/jit(_where)/select_n | solution.py:18
  66.3 0.0 all-reduce.3.cloned.1.call-update
  66.4 0.0 all-gather.5.cloned.1.call-start
  66.4 165.1 %all-reduce.3.cloned.1.call-done = (bf16[256,6144]{0,1:T(8,128)(2,1)}, bf16[256,6144]{0,1:T(8,128)(2,1)}) async-done(((bf16[256,6144]{0,1:T(8,128)(2,1)}, bf16[256,6144]{0,1:T(8,128)(2,1)}), (bf16[256,6144]{0,1:T(8,128)(2,1)}, bf16[256,6144]{0,1:T(8,128)(2,1)})) %all-reduce.3.cloned.1.call-update) | async-done | bytes 6291472 | tf_op jit(solution)/shard_map/psum | solution.py:18
  231.5 0.0 all-gather.5.cloned.1.call-update
  231.5 0.0 all-gather.3.cloned.1.call-start
  231.5 0.7 all-gather.3.cloned.1.call-update
  232.2 23.8 %all-gather.5.cloned.1.call-done = bf16[512,6144]{0,1:T(8,128)(2,1)} async-done(((bf16[256,6144]{0,1:T(8,128)(2,1)}), bf16[512,6144]{0,1:T(8,128)(2,1)}) %all-gather.5.cloned.1.call-update) | async-done | bytes 6291472 | tf_op jit(solution)/shard_map/all_gather | solution.py:37
  256.0 5.4 %fusion.1 = f32[512,256]{1,0:T(8,128)} fusion(bf16[512,6144]{0,1:T(8,128)(2,1)} %all-gather.5.cloned.1.call-done, bf16[256,6144]{0,1:T(8,128)(2,1)S(1)} %bitcast.12), kind=kOutput, calls=%fused_computation.5 | convolution fusion | flops 1610612736 | bytes 9961472 | tf_op jit(solution)/shard_map/dot_general | solution.py:22
  261.4 18.7 %all-gather.3.cloned.1.call-done = bf16[512,6144]{0,1:T(8,128)(2,1)} async-done(((bf16[256,6144]{0,1:T(8,128)(2,1)}), bf16[512,6144]{0,1:T(8,128)(2,1)}) %all-gather.3.cloned.1.call-update) | async-done | bytes 6291472 | tf_op jit(solution)/shard_map/all_gather | solution.py:37
  280.1 0.0 copy-start
  280.1 4.7 %fusion = f32[512,256]{1,0:T(8,128)S(1)} fusion(bf16[512,6144]{0,1:T(8,128)(2,1)} %all-gather.3.cloned.1.call-done, bf16[256,6144]{0,1:T(8,128)(2,1)S(1)} %bitcast.13), kind=kOutput, calls=%fused_computation.4 | convolution fusion | flops 1610612736 | bytes 9961472 | tf_op jit(solution)/shard_map/dot_general | solution.py:22
  284.8 0.0 copy-done
  284.8 1.1 maximum_multiply_fusion
Async XLA Ops:
  17.5 42.4 %all-to-all-start.1 = ((bf16[8,256,768]{2,1,0:T(8,128)(2,1)}), bf16[8,256,768]{2,1,0:T(8,128)(2,1)}, u32[]{:S(2)}, u32[]{:S(2)}) async-start(bf16[8,256,768]{2,1,0:T(8,128)(2,1)} %stack.5), calls=%async_computation.1 | async-start | bytes 6291456 | tf_op jit(solution)/shard_map/all_to_all | solution.py:12
  22.4 209.1 %all-reduce.3.cloned.1.call-start = ((), (), s32[]{:S(2)}) async-start(), calls=%async_computation.4 | async-start | bytes 12582912 | tf_op jit(solution)/shard_map/psum | solution.py:18
  66.4 189.6 %all-gather.5.cloned.1.call-start = ((), (), s32[]{:S(2)}) async-start(), calls=%async_computation.3 | async-start | bytes 9437184 | tf_op jit(solution)/shard_map/all_gather | solution.py:37
  231.5 48.6 %all-gather.3.cloned.1.call-start = ((), (), s32[]{:S(2)}) async-start(), calls=%async_computation.2 | async-start | bytes 9437184 | tf_op jit(solution)/shard_map/all_gather | solution.py:37
  280.1 4.7 %copy-start = (f32[512,256]{1,0:T(8,128)S(1)}, f32[512,256]{1,0:T(8,128)}, u32[]{:S(2)}) copy-start(f32[512,256]{1,0:T(8,128)} %fusion.1) | copy-start | bytes 1572868
Sparse Core Ops, SparseCore 0:
  66.5 164.9 all-reduce.2
  233.3 22.6 all-gather.4
  257.8 22.2 all-gather.2
